TPU v7x, 32 devices: a whole 2x2x4 slice. The times are simulated.
32 devices in a mesh: atoms: 8 (over z, y), sig: 4 (over x, core).
Axes of the slice: x: 2, y: 2, z: 4, core: 2. Of those that a mesh axis runs over, the one named last changes fastest.
Arguments:
- signals: bfloat16 [1024, 512], P(None, 'sig'), may hold values from -6 to 6
- dictionary: bfloat16 [1024, 4096], P(None, ('atoms', 'sig')), may hold values from -0.1875 to 0.1875
- selected: int32 [2, 4], P(None, 'sig'), may hold values from 0 to 63
- inverses: bfloat16 [2, 4, 64, 64], P(None, 'sig'), may hold values from -0.14 to 1.14
Outputs:
- correlations: bfloat16 [4096, 512], P('atoms', 'sig')
- coefficients: bfloat16 [2, 64, 512], P(None, None, 'sig')
- peak: float32 [512], P('sig')
All inputs are finite; a program needn't handle non-finite values.
Results may differ from a plain program's by a relative error of at most 0.006.
Values may be sent and summed in bfloat16 or wider, within the bound.
No kernel may reach another device: no remote copies, remote signals or barrier semaphores. Data moves between devices by JAX's collectives and lax.ppermute only.
A program may use at most 128 MiB of HBM per device.

v0:
```python
import jax
import jax.numpy as jnp
from jax import lax
from jax.sharding import PartitionSpec as P

BLK = 64
SB = 128
STEPS = 2


def spread(block, axis, holder):
    block = jnp.where(lax.axis_index(axis) == holder, block, jnp.zeros_like(block))
    return lax.psum(block, axis)


def shards(signals, dictionary, selected, inverses):
    gathered = lax.all_gather(dictionary, "sig", axis=1, tiled=True)
    width = gathered.shape[1]
    blocks_here = width // BLK
    block_total = signals.shape[1] // SB
    correlation = lax.dot_general(
        gathered, signals, (((0,), (0,)), ((), ())), preferred_element_type=jnp.float32
    )
    coefficients = jnp.zeros((STEPS, BLK, signals.shape[1]), jnp.bfloat16)

    def locate(step, slot):
        block_id = selected[step, slot]
        owner_index = block_id // blocks_here
        offset = block_id % blocks_here * BLK
        return (owner_index, offset)

    def panel_of(atom_block):
        return lax.dot_general(
            gathered, atom_block, (((0,), (0,)), ((), ())), preferred_element_type=jnp.float32
        ).astype(jnp.bfloat16)

    def refit(step, slot, rows_block):
        return jnp.dot(
            inverses[step, slot].astype(jnp.float32),
            rows_block,
            precision=lax.Precision.HIGHEST,
            preferred_element_type=jnp.float32,
        ).astype(jnp.bfloat16)

    def solve_block(correlation, step, slot, offset):
        rows_block = lax.dynamic_slice(correlation, (offset, slot * SB), (BLK, SB))
        return refit(step, slot, rows_block)

    def apply_block(correlation, coefficients, gram_panel, weights_block, step, slot):
        column_start = slot * SB
        columns = correlation
        columns = columns - jnp.dot(gram_panel, weights_block, preferred_element_type=jnp.float32)
        correlation = columns
        coefficients = lax.dynamic_update_slice(
            coefficients, weights_block[None], (step, 0, column_start)
        )
        return (correlation, coefficients)

    for step in range(STEPS):

        def advance(slot, carried):
            correlation, coefficients = carried
            owner_index, offset = locate(step, slot)
            atom_block = lax.dynamic_slice_in_dim(gathered, offset, BLK, 1)
            weights_block = solve_block(correlation, step, slot, offset)
            atom_block, weights_block = (
                spread(atom_block, "atoms", owner_index),
                spread(weights_block, "atoms", owner_index),
            )
            gram_panel = panel_of(atom_block)
            return apply_block(correlation, coefficients, gram_panel, weights_block, step, slot)

        correlation, coefficients = lax.fori_loop(
            0, block_total, advance, (correlation, coefficients)
        )
    largest = lax.pmax(jnp.max(jnp.abs(correlation), axis=0), "atoms")
    return (correlation.astype(jnp.bfloat16), coefficients, largest)


def solution(mesh):
    placed = (P(None, "sig"), P(None, ("atoms", "sig")), P(None, "sig"), P(None, "sig", None, None))
    return jax.shard_map(
        shards,
        mesh=mesh,
        in_specs=placed,
        out_specs=(P("atoms", "sig"), P(None, None, "sig"), P("sig")),
        check_vma=False,
    )
```

profile of v0, /device:TPU:0, one launch (start us, length us, event | category | flops | bytes accessed | tf_op | source)
XLA Modules:
  0.0 168.5 jit_solution(2854032412302445752)
XLA Ops:
  7.2 0.0 copy-start
  7.2 0.0 copy-start.4
  7.2 0.0 all-gather.2.cloned.1.call-start
  7.2 0.7 all-gather.2.cloned.1.call-update
  7.9 0.0 all-reduce.3.cloned.1.call-start
  8.0 0.0 copy-done.4
  8.0 0.6 fusion.12
  13.8 15.3 %all-gather.2.cloned.1.call-done = bf16[1024,512]{1,0:T(8,128)(2,1)} async-done(((bf16[1024,128]{1,0:T(8,128)(2,1)}), bf16[1024,512]{1,0:T(8,128)(2,1)}) %all-gather.2.cloned.1.call-update) | async-done | bytes 1048592 | tf_op jit(solution)/shard_map/all_gather | solution.py:17
  29.1 0.0 copy-start.1
  29.2 2.2 %dynamic-slice_select_fusion = (bf16[1024,64]{1,0:T(8,128)(2,1)}, bf16[1024,64]{1,0:T(8,128)(2,1)}) fusion(bf16[1024,512]{1,0:T(8,128)(2,1)} %all-gather.2.cloned.1.call-done, s32[]{:T(128)S(6)} %select_n.99, pred[]{:T(512)S(6)} %eq.16, s32[]{:T(128)S(6)} %select_n.91, pred[]{:T(512)S(6)} %eq.15), kind=kLoop, calls=%fused_computation.11 | loop fusion | flops 131072 | bytes 524298 | tf_op jit(solution)/shard_map/while/body/eval_jaxpr/jit(_where)/select_n | solution.py:12
  31.3 0.0 all-reduce.3.cloned.1.call-update
  31.3 0.0 copy-done
  31.3 0.0 copy-done.1
  31.4 0.0 copy-start.3
  31.4 0.5 fusion.13
  31.8 0.3 copy-done.3
  32.1 0.2 fusion.1
  32.3 37.3 %psum.33 = bf16[64,128]{1,0:T(8,128)(2,1)S(1)} all-reduce(bf16[64,128]{1,0:T(8,128)(2,1)S(1)} %fusion.1), channel_id=1, replica_groups=mesh['atoms'=8,'sig'=4] {'atoms'}, use_global_device_ids=true, to_apply=%region_1.2 | all-reduce | flops 8192 | bytes 32768 | tf_op jit(solution)/shard_map/while/body/eval_jaxpr/psum | solution.py:13
  69.5 35.7 %all-reduce.3.cloned.1.call-done = (bf16[1024,64]{1,0:T(8,128)(2,1)}, bf16[1024,64]{1,0:T(8,128)(2,1)}) async-done(((bf16[1024,64]{1,0:T(8,128)(2,1)}, bf16[1024,64]{1,0:T(8,128)(2,1)}), (bf16[1024,64]{1,0:T(8,128)(2,1)}, bf16[1024,64]{1,0:T(8,128)(2,1)})) %all-reduce.3.cloned.1.call-update) | async-done | bytes 262160 | tf_op jit(solution)/shard_map/while/body/eval_jaxpr/psum | solution.py:13
  105.2 0.0 copy-start.2
  105.2 1.5 convolution_subtract_fusion.1
  106.7 0.2 fusion.3
  106.9 35.4 %psum.35 = bf16[64,128]{1,0:T(8,128)(2,1)S(1)} all-reduce(bf16[64,128]{1,0:T(8,128)(2,1)S(1)} %fusion.3), channel_id=1, replica_groups=mesh['atoms'=8,'sig'=4] {'atoms'}, use_global_device_ids=true, to_apply=%region_3.4 | all-reduce | flops 8192 | bytes 32768 | tf_op jit(solution)/shard_map/while/body/eval_jaxpr/psum | solution.py:13
  142.3 0.0 copy-done.2
  142.3 1.2 abs_reduce_fusion
  143.4 17.6 %pmax.7 = f32[128]{0:T(128)} all-reduce(f32[128]{0:T(128)S(1)} %get-tuple-element.42), channel_id=1, replica_groups=mesh['atoms'=8,'sig'=4] {'atoms'}, use_global_device_ids=true, to_apply=%region_5.6 | all-reduce | flops 128 | bytes 1024 | tf_op jit(solution)/shard_map/pmax | solution.py:76
  161.1 0.6 pad_maximum_fusion
Async XLA Ops:
  7.2 24.2 %copy-start = (bf16[1024,128]{1,0:T(8,128)(2,1)S(1)}, bf16[1024,128]{1,0:T(8,128)(2,1)}, u32[]{:S(2)}) copy-start(bf16[1024,128]{1,0:T(8,128)(2,1)} %param.4) | copy-start | bytes 786436
  7.2 0.8 copy-start.4
  7.2 22.0 %all-gather.2.cloned.1.call-start = ((), (), s32[]{:S(2)}) async-start(), calls=%async_computation | async-start | bytes 1310720 | tf_op jit(solution)/shard_map/all_gather | solution.py:17
  7.9 97.3 %all-reduce.3.cloned.1.call-start = ((), (), s32[]{:S(2)}) async-start(), calls=%async_computation.1 | async-start | bytes 1048576 | tf_op jit(solution)/shard_map/while/body/eval_jaxpr/psum | solution.py:13
  29.1 2.2 %copy-start.1 = (bf16[1024,512]{1,0:T(8,128)(2,1)S(1)}, bf16[1024,512]{1,0:T(8,128)(2,1)}, u32[]{:S(2)}) copy-start(bf16[1024,512]{1,0:T(8,128)(2,1)} %all-gather.2.cloned.1.call-done) | copy-start | bytes 3145732
  31.4 0.8 copy-start.3
  105.2 37.0 %copy-start.2 = (bf16[1024,64]{1,0:T(8,128)(2,1)S(1)}, bf16[1024,64]{1,0:T(8,128)(2,1)}, u32[]{:S(2)}) copy-start(bf16[1024,64]{1,0:T(8,128)(2,1)} %get-tuple-element.32) | copy-start | bytes 393220
Sparse Core Ops, SparseCore 0:
  9.6 19.5 all-gather.1
  32.6 72.5 all-reduce.2
where the time goes:
time: 169 us
  blocking collectives  90.2 us (53%)
  waiting for transfers between devices  51.7 us (31%)
  between operations  19.3 us (11%)
  matrix products  3.47 us (2%)
  other arithmetic  2.78 us (2%)
    psum x2, blocking collectives, spread(): return lax.psum(block, axis)  72.6 us
    psum x1, waiting for transfers between devices, spread(): return lax.psum(block, axis)  35.7 us
    pmax x1, blocking collectives, shards(): largest = lax.pmax(jnp.max(jnp.abs(correlation), axis=0), 'atoms')  17.6 us
    all_gather x1, waiting for transfers between devices, shards(): gathered = lax.all_gather(dictionary, 'sig', axis=1, tiled=True)  15.3 us
  transfers between devices with their start and end apart: 2, of which 2 were waited for; matrix products, arithmetic and copies ran while one was open for 1% of the time, Pallas kernels for 0%

commit v1 on v0

--- a/solution.py
+++ b/solution.py
@@ -10,7 +10,7 @@
 
 def spread(block, axis, holder):
     block = jnp.where(lax.axis_index(axis) == holder, block, jnp.zeros_like(block))
-    return lax.psum(block, axis)
+    return jnp.sum(lax.all_gather(block, axis), axis=0)
 
 
 def shards(signals, dictionary, selected, inverses):

time: 169 us -> 162 us (0.959)
  blocking collectives: 90.2 us -> 81.6 us
  other arithmetic: 2.78 us -> 6.93 us
  waiting for transfers between devices: 51.7 us -> 48.4 us
    psum x2 -> x0, blocking collectives: 72.6 us -> none  [spread(): return lax.psum(block, axis)]
    all_gather x0 -> x2, blocking collectives: none -> 61.7 us  [spread(): return jnp.sum(lax.all_gather(block, axis), axis=0)]
    psum x1 -> x0, waiting for transfers between devices: 35.7 us -> none  [spread(): return lax.psum(block, axis)]
    all_gather x0 -> x2, waiting for transfers between devices: none -> 32.4 us  [spread(): return jnp.sum(lax.all_gather(block, axis), axis=0)]
    reduce_sum x0 -> x4, other arithmetic: none -> 4.27 us  [spread(): return jnp.sum(lax.all_gather(block, axis), axis=0)]
    pmax x1, blocking collectives: 17.6 us -> 19.9 us  [shards(): largest = lax.pmax(jnp.max(jnp.abs(correlation), axis=0), 'atoms')]
  transfers between devices with their start and end apart: 2 -> 3, of which waited for: 2 -> 3; matrix products, arithmetic and copies ran while one was open for 1% -> 4% of each run, Pallas kernels for 0% -> 0%
where the time goes in v1:
time: 162 us; the launch traced here: 161 us
  blocking collectives  81.6 us (50%)
  waiting for transfers between devices  48.4 us (30%)
  between operations  19.1 us (12%)
  other arithmetic  6.93 us (4%)
  matrix products  3.8 us (2%)
    all_gather x2, blocking collectives, spread(): return jnp.sum(lax.all_gather(block, axis), axis=0)  61.7 us
    all_gather x2, waiting for transfers between devices, spread(): return jnp.sum(lax.all_gather(block, axis), axis=0)  32.4 us
    pmax x1, blocking collectives, shards(): largest = lax.pmax(jnp.max(jnp.abs(correlation), axis=0), 'atoms')  19.9 us
    all_gather x1, waiting for transfers between devices, shards(): gathered = lax.all_gather(dictionary, 'sig', axis=1, tiled=True)  14.6 us
    reduce_sum x4, other arithmetic, spread(): return jnp.sum(lax.all_gather(block, axis), axis=0)  4.27 us
  transfers between devices with their start and end apart: 3, of which 3 were waited for; matrix products, arithmetic and copies ran while one was open for 4% of the time, Pallas kernels for 0%

profile of v1, /device:TPU:0, one launch (start us, length us, event | category | flops | bytes accessed | tf_op | source)
XLA Modules:
  0.0 161.2 jit_solution(10532862490577517941)
XLA Ops:
  7.2 0.0 copy-start
  7.2 0.0 copy-start.2
  7.2 0.0 all-gather.8.cloned.1.call-start
  7.2 0.7 all-gather.8.cloned.1.call-update
  7.9 0.0 all-gather.10.cloned.1.call-start
  8.0 1.3 fusion.12
  14.5 14.6 %all-gather.8.cloned.1.call-done = bf16[1024,512]{1,0:T(8,128)(2,1)} async-done(((bf16[1024,128]{1,0:T(8,128)(2,1)}), bf16[1024,512]{1,0:T(8,128)(2,1)}) %all-gather.8.cloned.1.call-update) | async-done | bytes 1048592 | tf_op jit(solution)/shard_map/all_gather | solution.py:17
  29.1 2.0 %dynamic-slice_select_fusion = (bf16[1024,64]{1,0:T(8,128)(2,1)}, bf16[1024,64]{1,0:T(8,128)(2,1)}) fusion(bf16[1024,512]{1,0:T(8,128)(2,1)} %all-gather.8.cloned.1.call-done, s32[]{:T(128)S(6)} %select_n.99, pred[]{:T(512)S(6)} %eq.16, s32[]{:T(128)S(6)} %select_n.91, pred[]{:T(512)S(6)} %eq.15), kind=kLoop, calls=%fused_computation.11 | loop fusion | flops 131072 | bytes 524298 | tf_op jit(solution)/shard_map/while/body/eval_jaxpr/jit(_where)/select_n | solution.py:12
  31.2 0.0 all-gather.10.cloned.1.call-update
  31.2 0.0 all-gather.12.cloned.1.call-start
  31.3 0.7 all-gather.12.cloned.1.call-update
  32.0 0.0 copy-done
  32.0 0.0 copy-start.1
  32.0 1.8 %fusion.13 = f32[512,128]{1,0:T(8,128)S(1)} fusion(bf16[1024,512]{1,0:T(8,128)(2,1)} %all-gather.8.cloned.1.call-done, bf16[1024,128]{1,0:T(8,128)(2,1)S(1)} %copy-done), kind=kOutput, calls=%fused_computation.23 | convolution fusion | flops 134217728 | bytes 1572864 | tf_op jit(solution)/shard_map/dot_general | solution.py:21
  33.8 0.0 copy-done.2
  33.8 0.2 fusion.1
  33.9 30.8 %all-gather.1 = bf16[512,128]{1,0:T(8,128)(2,1)S(1)} all-gather(bf16[64,128]{1,0:T(8,128)(2,1)S(1)} %fusion.1), channel_id=3, replica_groups=mesh['atoms'=8,'sig'=4] {'atoms'}, dimensions={0}, use_global_device_ids=true | all-gather | bytes 147456 | tf_op jit(solution)/shard_map/while/body/eval_jaxpr/all_gather | solution.py:13
  64.8 15.7 %all-gather.10.cloned.1.call-done = bf16[8192,64]{1,0:T(8,128)(2,1)} async-done(((bf16[1024,64]{1,0:T(8,128)(2,1)}), bf16[8192,64]{1,0:T(8,128)(2,1)}) %all-gather.10.cloned.1.call-update) | async-done | bytes 1048592 | tf_op jit(solution)/shard_map/while/body/eval_jaxpr/all_gather | solution.py:13
  80.5 2.1 %reduce_sum.52 = bf16[1024,64]{1,0:T(8,128)(2,1)S(1)} reduce(bf16[8,1024,64]{2,1,0:T(8,128)(2,1)} %bitcast.27, bf16[]{:T(256)} %constant.95.clone.1), dimensions={0}, to_apply=%region_0.1 | reduce | flops 458752 | bytes 1179650 | tf_op jit(solution)/shard_map/while/body/eval_jaxpr/reduce_sum | solution.py:13
  82.6 0.0 copy-done.1
  82.6 0.5 convolution_subtract_fusion.1
  83.2 0.2 fusion.3
  83.3 30.9 %all-gather.3 = bf16[512,128]{1,0:T(8,128)(2,1)S(1)} all-gather(bf16[64,128]{1,0:T(8,128)(2,1)S(1)} %fusion.3), channel_id=5, replica_groups=mesh['atoms'=8,'sig'=4] {'atoms'}, dimensions={0}, use_global_device_ids=true | all-gather | bytes 147456 | tf_op jit(solution)/shard_map/while/body/eval_jaxpr/all_gather | solution.py:13
  114.2 16.7 %all-gather.12.cloned.1.call-done = bf16[8192,64]{1,0:T(8,128)(2,1)} async-done(((bf16[1024,64]{1,0:T(8,128)(2,1)}), bf16[8192,64]{1,0:T(8,128)(2,1)}) %all-gather.12.cloned.1.call-update) | async-done | bytes 1048592 | tf_op jit(solution)/shard_map/while/body/eval_jaxpr/all_gather | solution.py:13
  130.9 2.1 %reduce_sum.54 = bf16[1024,64]{1,0:T(8,128)(2,1)S(1)} reduce(bf16[8,1024,64]{2,1,0:T(8,128)(2,1)} %bitcast.26, bf16[]{:T(256)} %constant.95.clone.1), dimensions={0}, to_apply=%region_2.3 | reduce | flops 458752 | bytes 1179650 | tf_op jit(solution)/shard_map/while/body/eval_jaxpr/reduce_sum | solution.py:13
  133.0 1.2 abs_reduce_fusion
  134.2 19.9 %pmax.7 = f32[128]{0:T(128)} all-reduce(f32[128]{0:T(128)S(1)} %get-tuple-element.33), channel_id=1, replica_groups=mesh['atoms'=8,'sig'=4] {'atoms'}, use_global_device_ids=true, to_apply=%region_5.6 | all-reduce | flops 128 | bytes 1024 | tf_op jit(solution)/shard_map/pmax | solution.py:76
  154.0 0.6 pad_maximum_fusion
  (2 shorter events, 0.0 us)
Async XLA Ops:
  7.2 24.8 %copy-start = (bf16[1024,128]{1,0:T(8,128)(2,1)S(1)}, bf16[1024,128]{1,0:T(8,128)(2,1)}, u32[]{:S(2)}) copy-start(bf16[1024,128]{1,0:T(8,128)(2,1)} %param.4) | copy-start | bytes 786436
  7.2 26.6 %copy-start.2 = (bf16[2,1,64,64]{3,2,1,0:T(8,128)(2,1)S(1)}, bf16[2,1,64,64]{3,2,1,0:T(8,128)(2,1)}, u32[]{:S(2)}) copy-start(bf16[2,1,64,64]{3,2,1,0:T(8,128)(2,1)} %param.7) | copy-start | bytes 49156
  7.2 22.0 %all-gather.8.cloned.1.call-start = ((), (), s32[]{:S(2)}) async-start(), calls=%async_computation | async-start | bytes 1310720 | tf_op jit(solution)/shard_map/all_gather | solution.py:17
  7.9 72.6 %all-gather.10.cloned.1.call-start = ((), (), s32[]{:S(2)}) async-start(), calls=%async_computation.1 | async-start | bytes 2359296 | tf_op jit(solution)/shard_map/while/body/eval_jaxpr/all_gather | solution.py:13
  31.2 99.6 %all-gather.12.cloned.1.call-start = ((), (), s32[]{:S(2)}) async-start(), calls=%async_computation.2 | async-start | bytes 2359296 | tf_op jit(solution)/shard_map/while/body/eval_jaxpr/all_gather | solution.py:13
  32.0 50.7 %copy-start.1 = (bf16[1024,512]{1,0:T(8,128)(2,1)S(1)}, bf16[1024,512]{1,0:T(8,128)(2,1)}, u32[]{:S(2)}) copy-start(bf16[1024,512]{1,0:T(8,128)(2,1)} %all-gather.8.cloned.1.call-done) | copy-start | bytes 3145732
Sparse Core Ops, SparseCore 0:
  9.6 19.5 all-gather.7
  31.3 49.1 all-gather.9
  82.6 48.1 all-gather.11
